TPU v7x, 256 devices: a whole 4x4x8 slice. The times are simulated.
256 devices in a mesh: row: 16 (over y, x), col: 16 (over z, core).
Axes of the slice: x: 4, y: 4, z: 8, core: 2. Of those that a mesh axis runs over, the one named last changes fastest.
Arguments:
- rhs: float32 [128, 32768], P('row', 'col'), may hold values from -60 to 60
- flex_tiles: float32 [131072, 2048], P('row', 'col'), may hold values from -0.25 to 0.25
- flex_cols: int32 [256, 64], P('row', 'col'), may hold values from 0 to 15, as said below
- stiff_tiles: float32 [131072, 2048], P('row', 'col'), may hold values from -0.25 to 0.25
- stiff_cols: int32 [256, 64], P('row', 'col'), may hold values from 0 to 15, as said below
- deflation: float32 [512, 32768], P('row', 'col'), may hold values from -0.375 to 0.375
- coarse_rows: float32 [8192, 8192], P(('row', 'col')), may hold values from -5 to 5, as said below
- face_rows: int32 [64, 2048], P('row', 'col'), may hold values from 0 to 2047, as said below
- face_len: int32 [16, 64], P('row', 'col'), may hold values from 0 to 128, as said below
Outputs:
- solution: float32 [128, 32768], P('row', 'col')
- residual: float32 [128, 32768], P('row', 'col')
- correction: float32 [128, 32768], P('row', 'col')
Inputs may be any that keep to these rules, and one draw needn't show every extreme that they name: `flex_cols`: row b of a subdomain's block list names 4 different block columns, the first being b. `stiff_cols`: row b of a subdomain's block list names 4 different block columns, the first being b. `coarse_rows`: the whole matrix is symmetric. `face_rows`: the four lists of a subdomain name 512 different multipliers of it. `face_len`: the two subdomains of a face give it the same length; faces on the grid's boundary have length 0, inner faces at least 32.
All inputs are finite; a program needn't handle non-finite values.
Results may differ from a plain program's by a relative error of at most 0.0003.
Values sent between devices are 32-bit elements; how exact they have to be, the bound alone decides.
A program may use at most 64 MiB of HBM per device.

v0:
```python
import jax
import jax.numpy as jnp
from jax import lax
from jax.sharding import PartitionSpec as P

ITERS = 3
PRECISE = lax.Precision.HIGHEST


def with_halo(cells, sides, width):
    for axis, dim in sides:
        count = lax.axis_size(axis)
        ends = count - 1
        head = lax.slice_in_dim(cells, 0, width, axis=dim)
        tail = lax.slice_in_dim(cells, cells.shape[dim] - width, cells.shape[dim], axis=dim)
        cells = jnp.concatenate(
            [
                lax.ppermute(tail, axis, [(i, (i + 1) % count) for i in range(ends)]),
                cells,
                lax.ppermute(head, axis, [((i + 1) % count, i) for i in range(ends)]),
            ],
            axis=dim,
        )
    return cells


def sparse_forward(vector, tile_set, columns):
    load_count = vector.shape[0]
    blocks, per_row = columns.shape
    tile_width = tile_set.shape[-1]
    pieces = vector.reshape(load_count, blocks, tile_width)
    picked = jnp.take(pieces, columns.reshape(-1), axis=1).reshape(
        load_count, blocks, per_row, tile_width
    )
    product = jnp.einsum("lbkw,bkwv->lbv", picked, tile_set, precision=PRECISE)
    return product.reshape(load_count, blocks * tile_width)


def sparse_backward(vector, tile_set, columns):
    load_count = vector.shape[0]
    blocks, per_row = columns.shape
    tile_width = tile_set.shape[-1]
    pieces = vector.reshape(load_count, blocks, tile_width)
    product = jnp.einsum("lbv,bkwv->lbkw", pieces, tile_set, precision=PRECISE)
    onehot = (columns[:, :, None] == jnp.arange(blocks, dtype=jnp.int32)[None, None, :]).astype(
        jnp.float32
    )
    summed = jnp.einsum("lbkw,bkj->ljw", product, onehot, precision=PRECISE)
    return summed.reshape(load_count, blocks * tile_width)


def pair_totals(first_field, second_field, third_field, fourth_field):
    return lax.psum(
        (jnp.sum(first_field * second_field, axis=1), jnp.sum(third_field * fourth_field, axis=1)),
        ("row", "col"),
    )


def shards(
    rhs, flex_tiles, flex_cols, stiff_tiles, stiff_cols, deflation, coarse_rows, face_rows, face_len
):
    blocks, per_row = flex_cols.shape
    tile_width = flex_tiles.shape[1]
    flex_set = flex_tiles.reshape(blocks, per_row, tile_width, tile_width)
    stiff_set = stiff_tiles.reshape(blocks, per_row, tile_width, tile_width)
    face_width = face_rows.shape[1]
    flat_index = face_rows.reshape(-1)
    slots = jnp.arange(face_width, dtype=jnp.int32)
    live_mask = (slots[None, :] < face_len.reshape(4, 1)).astype(jnp.float32)

    def face_part(vector):
        load_count = vector.shape[0]
        traces = jnp.take(vector, flat_index, axis=1).reshape(load_count, 4, face_width)
        across_rows = with_halo(traces[:, 0:2], (("row", 1),), 1)
        across_cols = with_halo(traces[:, 2:4], (("col", 1),), 1)
        partner = jnp.stack(
            [across_rows[:, 0], across_rows[:, 3], across_cols[:, 0], across_cols[:, 3]], axis=1
        )
        jump_values = (traces - partner) * live_mask[None]
        return (
            jnp.zeros_like(vector)
            .at[:, flat_index]
            .add(jump_values.reshape(load_count, 4 * face_width))
        )

    def operate(vector):
        coupling = face_part(vector)
        after_flex = sparse_forward(vector, flex_set, flex_cols)
        after_stiff = sparse_forward(after_flex, stiff_set, stiff_cols)
        back_stiff = sparse_backward(after_stiff, stiff_set, stiff_cols)
        local_part = sparse_backward(back_stiff, flex_set, flex_cols)
        return vector + local_part + coupling

    def precondition(vector):
        coefficients = jnp.einsum("lm,dm->ld", vector, deflation, precision=PRECISE)
        energy = jnp.einsum(
            "ln,dn->ld",
            lax.all_gather(coefficients, ("row", "col"), axis=1, tiled=True),
            coarse_rows,
            precision=PRECISE,
        )
        return vector + jnp.einsum("ld,dm->lm", energy, deflation, precision=PRECISE)

    residual = rhs
    solution = jnp.zeros_like(rhs)
    correction = precondition(residual)
    direction = correction
    image = operate(direction)
    curvature_sum, descent_sum = pair_totals(direction, image, residual, direction)
    for iteration in range(ITERS):
        step_size = (descent_sum / curvature_sum)[:, None]
        solution = solution + step_size * direction
        residual = residual - step_size * image
        correction = precondition(residual)
        if iteration + 1 < ITERS:
            cross_sum = lax.psum(jnp.sum(correction * image, axis=1), ("row", "col"))
            blend = -cross_sum / curvature_sum
            direction = correction + blend[:, None] * direction
            image = operate(direction)
            curvature_sum, descent_sum = pair_totals(direction, image, residual, direction)
    return (solution, residual, correction)


def solution(mesh):
    return jax.shard_map(
        shards,
        mesh=mesh,
        in_specs=(
            P("row", "col"),
            P("row", "col"),
            P("row", "col"),
            P("row", "col"),
            P("row", "col"),
            P("row", "col"),
            P(("row", "col"), None),
            P("row", "col"),
            P("row", "col"),
        ),
        out_specs=(P("row", "col"), P("row", "col"), P("row", "col")),
        check_vma=False,
    )
```

profile of v0, /device:TPU:1, one launch (start us, length us, event | category | flops | bytes accessed | tf_op | source)
XLA Modules:
  0.0 747.8 jit_solution(5366016694959184341)
XLA Ops:
  0.7 0.8 compare_select_fusion.1
  1.5 0.7 compare_and_fusion
  2.1 1.2 convolution_bitcast_fusion.21
  3.4 67.8 %all-gather = f32[256,32,8]{1,2,0:T(8,128)S(1)} all-gather(f32[1,32,8]{1,2,0:T(8,128)S(1)} %convolution_bitcast_fusion.21), channel_id=1, replica_groups=mesh['row'=16,'col'=16] {'row','col'}, dimensions={0}, use_global_device_ids=true | all-gather | bytes 263168 | tf_op jit(solution)/shard_map/all_gather | solution.py:98
  71.4 0.5 reshape.278
  71.9 0.9 fusion.36
  73.5 1.0 gather_fusion.2
  74.7 2.6 collective-permute-start
  77.4 1.3 collective-permute-start.1
  78.8 1.9 collective-permute-start.2
  80.8 2.7 collective-permute-start.3
  84.0 0.6 gather_fusion
  84.8 3.8 convolution_bitcast_fusion.17
  88.6 0.6 gather_fusion.1
  89.4 4.0 convolution_bitcast_fusion.16
  93.5 3.6 convolution_bitcast_fusion.5
  97.0 0.4 convolution_bitcast_fusion.11
  97.4 3.6 convolution_bitcast_fusion.4
  101.0 0.4 convolution_bitcast_fusion.10
  102.2 4.2 scatter_custom_fusion
  106.9 78.0 %all-reduce.2 = (f32[8]{0:T(128)S(1)}, f32[8]{0:T(128)S(1)}) all-reduce(f32[8]{0:T(128)S(1)} %get-tuple-element.10, f32[8]{0:T(128)S(1)} %get-tuple-element.9), channel_id=1, replica_groups=mesh['row'=16,'col'=16] {'row','col'}, use_global_device_ids=true, to_apply=%region_1.2 | all-reduce | flops 16 | bytes 128 | tf_op jit(solution)/shard_map/psum | solution.py:53
  185.2 60.6 %all-gather.1 = f32[256,32,8]{1,2,0:T(8,128)S(1)} all-gather(f32[1,32,8]{1,2,0:T(8,128)S(1)} %convolution_bitcast_fusion.20), channel_id=1, replica_groups=mesh['row'=16,'col'=16] {'row','col'}, dimensions={0}, use_global_device_ids=true | all-gather | bytes 263168 | tf_op jit(solution)/shard_map/all_gather | solution.py:98
  246.1 0.5 reshape.280
  246.5 0.9 fusion.37
  247.8 75.0 %psum.58 = f32[8]{0:T(128)S(1)} all-reduce(f32[8]{0:T(128)S(1)} %get-tuple-element.31), channel_id=1, replica_groups=mesh['row'=16,'col'=16] {'row','col'}, use_global_device_ids=true, to_apply=%region_6.9 | all-reduce | flops 8 | bytes 64 | tf_op jit(solution)/shard_map/psum | solution.py:116
  323.3 1.0 gather_fusion.5
  324.6 1.6 collective-permute-start.4
  326.2 1.3 collective-permute-start.5
  327.5 4.5 collective-permute-start.6
  332.1 2.1 collective-permute-start.7
  334.2 0.6 gather_fusion.3
  335.0 3.8 convolution_bitcast_fusion.15
  338.9 0.6 gather_fusion.4
  339.7 4.0 convolution_bitcast_fusion.14
  343.7 3.6 convolution_bitcast_fusion.3
  347.2 0.4 convolution_bitcast_fusion.9
  347.6 3.6 convolution_bitcast_fusion.2
  351.2 0.4 convolution_bitcast_fusion.8
  352.4 3.9 scatter_custom_fusion.1
  356.8 77.0 %all-reduce.1 = (f32[8]{0:T(128)S(1)}, f32[8]{0:T(128)S(1)}) all-reduce(f32[8]{0:T(128)S(1)} %get-tuple-element.8, f32[8]{0:T(128)S(1)} %get-tuple-element.7), channel_id=1, replica_groups=mesh['row'=16,'col'=16] {'row','col'}, use_global_device_ids=true, to_apply=%region_8.11 | all-reduce | flops 16 | bytes 128 | tf_op jit(solution)/shard_map/psum | solution.py:53
  434.1 61.9 %all-gather.2 = f32[256,32,8]{1,2,0:T(8,128)S(1)} all-gather(f32[1,32,8]{1,2,0:T(8,128)S(1)} %convolution_bitcast_fusion.19), channel_id=1, replica_groups=mesh['row'=16,'col'=16] {'row','col'}, dimensions={0}, use_global_device_ids=true | all-gather | bytes 263168 | tf_op jit(solution)/shard_map/all_gather | solution.py:98
  496.2 0.5 reshape.282
  496.7 0.9 fusion.38
  498.0 73.7 %psum.61 = f32[8]{0:T(128)S(1)} all-reduce(f32[8]{0:T(128)S(1)} %get-tuple-element.33), channel_id=1, replica_groups=mesh['row'=16,'col'=16] {'row','col'}, use_global_device_ids=true, to_apply=%region_13.16 | all-reduce | flops 8 | bytes 64 | tf_op jit(solution)/shard_map/psum | solution.py:116
  572.1 1.0 gather_fusion.8
  573.4 3.8 collective-permute-start.10
  577.3 1.9 collective-permute-start.11
  579.2 2.0 collective-permute-start.8
  581.3 1.7 collective-permute-start.9
  583.0 0.6 gather_fusion.6
  583.8 3.8 convolution_bitcast_fusion.13
  587.6 0.6 gather_fusion.7
  588.4 4.0 convolution_bitcast_fusion.12
  592.4 3.6 convolution_bitcast_fusion.1
  596.0 0.4 convolution_bitcast_fusion.7
  596.4 3.6 convolution_bitcast_fusion
  600.0 0.4 convolution_bitcast_fusion.6
  601.1 3.9 scatter_custom_fusion.2
  605.5 77.2 %all-reduce = (f32[8]{0:T(128)S(1)}, f32[8]{0:T(128)S(1)}) all-reduce(f32[8]{0:T(128)S(1)} %get-tuple-element.6, f32[8]{0:T(128)S(1)} %get-tuple-element.5), channel_id=1, replica_groups=mesh['row'=16,'col'=16] {'row','col'}, use_global_device_ids=true, to_apply=%region_15.18 | all-reduce | flops 16 | bytes 128 | tf_op jit(solution)/shard_map/psum | solution.py:53
  682.7 0.7 multiply_subtract_fusion
  683.7 61.3 %all-gather.3 = f32[256,32,8]{1,2,0:T(8,128)S(1)} all-gather(f32[1,32,8]{1,2,0:T(8,128)S(1)} %convolution_bitcast_fusion.18), channel_id=1, replica_groups=mesh['row'=16,'col'=16] {'row','col'}, dimensions={0}, use_global_device_ids=true | all-gather | bytes 263168 | tf_op jit(solution)/shard_map/all_gather | solution.py:98
  745.3 0.5 reshape.284
  745.8 0.9 fusion.39
  746.7 0.9 convolution_add_fusion
  (121 shorter events, 9.9 us)
Async XLA Ops:
  0.6 71.3 %copy-start = (f32[32,8192]{1,0:T(8,128)S(1)}, f32[32,8192]{1,0:T(8,128)}, u32[]{:S(2)}) copy-start(f32[32,8192]{1,0:T(8,128)} %param.19) | copy-start | bytes 3145732
  0.6 72.2 %copy-start.8 = (f32[8,2048]{1,0:T(8,128)S(1)}, f32[8,2048]{1,0:T(8,128)}, u32[]{:S(2)}) copy-start(f32[8,2048]{1,0:T(8,128)} %param.13) | copy-start | bytes 196612
  0.7 72.2 %copy-start.7 = (f32[32,2048]{1,0:T(8,128)S(1)}, f32[32,2048]{1,0:T(8,128)}, u32[]{:S(2)}) copy-start(f32[32,2048]{1,0:T(8,128)} %param.18) | copy-start | bytes 786436
  3.4 80.1 %copy-start.11 = (s32[16,4]{0,1:T(4,128)S(1)}, s32[16,4]{0,1:T(4,128)}, u32[]{:S(2)}) copy-start(s32[16,4]{0,1:T(4,128)} %param.15) | copy-start | bytes 772
  3.4 80.3 %copy-start.10 = (s32[16,4]{0,1:T(4,128)S(1)}, s32[16,4]{0,1:T(4,128)}, u32[]{:S(2)}) copy-start(s32[16,4]{0,1:T(4,128)} %param.17) | copy-start | bytes 772
  3.4 80.5 %copy-start.13 = (s32[1,4]{1,0:T(1,128)S(1)}, s32[1,4]{1,0:T(1,128)}, u32[]{:S(2)}) copy-start(s32[1,4]{1,0:T(1,128)} %param.21) | copy-start | bytes 52
  74.7 27.1 %collective-permute-start = (f32[8,1,128]{2,0,1:T(8,128)S(1)}, f32[8,1,128]{2,0,1:T(8,128)S(1)}, u32[]{:S(2)}, u32[]{:S(2)}) collective-permute-start(f32[8,1,128]{2,0,1:T(8,128)S(1)} %copy.118), channel_id=1, source_target_pairs={{0,16},{16,32},{32,48},{48,64},{64,80},{80,96},{96,112},{112,128},... | collective-permute-start | bytes 12296 | tf_op jit(solution)/shard_map/ppermute | solution.py:18
  77.4 24.4 %collective-permute-start.1 = (f32[8,1,128]{2,0,1:T(8,128)S(1)}, f32[8,1,128]{2,0,1:T(8,128)S(1)}, u32[]{:S(2)}, u32[]{:S(2)}) collective-permute-start(f32[8,1,128]{2,0,1:T(8,128)S(1)} %copy.119), channel_id=1, source_target_pairs={{16,0},{32,16},{48,32},{64,48},{80,64},{96,80},{112,96},{128,112},... | collective-permute-start | bytes 12296 | tf_op jit(solution)/shard_map/ppermute | solution.py:20
  78.8 23.0 %collective-permute-start.2 = (f32[8,1,128]{2,0,1:T(8,128)S(1)}, f32[8,1,128]{2,0,1:T(8,128)S(1)}, u32[]{:S(2)}, u32[]{:S(2)}) collective-permute-start(f32[8,1,128]{2,0,1:T(8,128)S(1)} %copy.120), channel_id=1, source_target_pairs={{0,1},{1,2},{2,3},{3,4},{4,5},{5,6},{6,7},{7,8},{8,9},{9,10},{10,1... | collective-permute-start | bytes 12296 | tf_op jit(solution)/shard_map/ppermute | solution.py:18
  80.8 21.1 %collective-permute-start.3 = (f32[8,1,128]{2,0,1:T(8,128)S(1)}, f32[8,1,128]{2,0,1:T(8,128)S(1)}, u32[]{:S(2)}, u32[]{:S(2)}) collective-permute-start(f32[8,1,128]{2,0,1:T(8,128)S(1)} %copy.121), channel_id=1, source_target_pairs={{1,0},{2,1},{3,2},{4,3},{5,4},{6,5},{7,6},{8,7},{9,8},{10,9},{11,1... | collective-permute-start | bytes 12296 | tf_op jit(solution)/shard_map/ppermute | solution.py:20
  89.3 4.2 copy-start.1
  89.4 8.0 %copy-start.4 = (f32[8192,128]{1,0:T(8,128)S(1)}, f32[8192,128]{1,0:T(8,128)}, u32[]{:S(2)}) copy-start(f32[8192,128]{1,0:T(8,128)} %param.14) | copy-start | bytes 12582916
  93.4 8.0 %copy-start.12 = (s32[4,128]{1,0:T(4,128)S(1)}, s32[4,128]{1,0:T(4,128)}, u32[]{:S(2)}) copy-start(s32[4,128]{1,0:T(4,128)} %param.20) | copy-start | bytes 6148
  324.6 27.4 %collective-permute-start.4 = (f32[8,1,128]{2,0,1:T(8,128)S(1)}, f32[8,1,128]{2,0,1:T(8,128)S(1)}, u32[]{:S(2)}, u32[]{:S(2)}) collective-permute-start(f32[8,1,128]{2,0,1:T(8,128)S(1)} %copy.122), channel_id=1, source_target_pairs={{0,16},{16,32},{32,48},{48,64},{64,80},{80,96},{96,112},{112,128},... | collective-permute-start | bytes 12296 | tf_op jit(solution)/shard_map/ppermute | solution.py:18
  326.2 25.8 %collective-permute-start.5 = (f32[8,1,128]{2,0,1:T(8,128)S(1)}, f32[8,1,128]{2,0,1:T(8,128)S(1)}, u32[]{:S(2)}, u32[]{:S(2)}) collective-permute-start(f32[8,1,128]{2,0,1:T(8,128)S(1)} %copy.123), channel_id=1, source_target_pairs={{16,0},{32,16},{48,32},{64,48},{80,64},{96,80},{112,96},{128,112},... | collective-permute-start | bytes 12296 | tf_op jit(solution)/shard_map/ppermute | solution.py:20
  327.5 24.5 %collective-permute-start.6 = (f32[8,1,128]{2,0,1:T(8,128)S(1)}, f32[8,1,128]{2,0,1:T(8,128)S(1)}, u32[]{:S(2)}, u32[]{:S(2)}) collective-permute-start(f32[8,1,128]{2,0,1:T(8,128)S(1)} %copy.124), channel_id=1, source_target_pairs={{0,1},{1,2},{2,3},{3,4},{4,5},{5,6},{6,7},{7,8},{8,9},{9,10},{10,1... | collective-permute-start | bytes 12296 | tf_op jit(solution)/shard_map/ppermute | solution.py:18
  332.1 19.9 %collective-permute-start.7 = (f32[8,1,128]{2,0,1:T(8,128)S(1)}, f32[8,1,128]{2,0,1:T(8,128)S(1)}, u32[]{:S(2)}, u32[]{:S(2)}) collective-permute-start(f32[8,1,128]{2,0,1:T(8,128)S(1)} %copy.125), channel_id=1, source_target_pairs={{1,0},{2,1},{3,2},{4,3},{5,4},{6,5},{7,6},{8,7},{9,8},{10,9},{11,1... | collective-permute-start | bytes 12296 | tf_op jit(solution)/shard_map/ppermute | solution.py:20
  339.5 4.2 copy-start.2
  339.6 8.0 %copy-start.5 = (f32[8192,128]{1,0:T(8,128)S(1)}, f32[8192,128]{1,0:T(8,128)}, u32[]{:S(2)}) copy-start(f32[8192,128]{1,0:T(8,128)} %param.14) | copy-start | bytes 12582916
  573.4 27.4 %collective-permute-start.10 = (f32[8,1,128]{2,0,1:T(8,128)S(1)}, f32[8,1,128]{2,0,1:T(8,128)S(1)}, u32[]{:S(2)}, u32[]{:S(2)}) collective-permute-start(f32[8,1,128]{2,0,1:T(8,128)S(1)} %copy.128), channel_id=1, source_target_pairs={{0,1},{1,2},{2,3},{3,4},{4,5},{5,6},{6,7},{7,8},{8,9},{9,10},{10,1... | collective-permute-start | bytes 12296 | tf_op jit(solution)/shard_map/ppermute | solution.py:18
  577.3 23.5 %collective-permute-start.11 = (f32[8,1,128]{2,0,1:T(8,128)S(1)}, f32[8,1,128]{2,0,1:T(8,128)S(1)}, u32[]{:S(2)}, u32[]{:S(2)}) collective-permute-start(f32[8,1,128]{2,0,1:T(8,128)S(1)} %copy.129), channel_id=1, source_target_pairs={{1,0},{2,1},{3,2},{4,3},{5,4},{6,5},{7,6},{8,7},{9,8},{10,9},{11,1... | collective-permute-start | bytes 12296 | tf_op jit(solution)/shard_map/ppermute | solution.py:20
  579.2 21.5 %collective-permute-start.8 = (f32[8,1,128]{2,0,1:T(8,128)S(1)}, f32[8,1,128]{2,0,1:T(8,128)S(1)}, u32[]{:S(2)}, u32[]{:S(2)}) collective-permute-start(f32[8,1,128]{2,0,1:T(8,128)S(1)} %copy.126), channel_id=1, source_target_pairs={{0,16},{16,32},{32,48},{48,64},{64,80},{80,96},{96,112},{112,128},... | collective-permute-start | bytes 12296 | tf_op jit(solution)/shard_map/ppermute | solution.py:18
  581.3 19.5 %collective-permute-start.9 = (f32[8,1,128]{2,0,1:T(8,128)S(1)}, f32[8,1,128]{2,0,1:T(8,128)S(1)}, u32[]{:S(2)}, u32[]{:S(2)}) collective-permute-start(f32[8,1,128]{2,0,1:T(8,128)S(1)} %copy.127), channel_id=1, source_target_pairs={{16,0},{32,16},{48,32},{64,48},{80,64},{96,80},{112,96},{128,112},... | collective-permute-start | bytes 12296 | tf_op jit(solution)/shard_map/ppermute | solution.py:20
  588.2 4.2 copy-start.3
  588.4 8.0 %copy-start.6 = (f32[8192,128]{1,0:T(8,128)S(1)}, f32[8192,128]{1,0:T(8,128)}, u32[]{:S(2)}) copy-start(f32[8192,128]{1,0:T(8,128)} %param.14) | copy-start | bytes 12582916
  683.5 64.1 %copy-start.9 = (f32[8,2048]{1,0:T(8,128)}, f32[8,2048]{1,0:T(8,128)S(1)}, u32[]{:S(2)}) copy-start(f32[8,2048]{1,0:T(8,128)S(1)} %get-tuple-element.29) | copy-start | bytes 196612
where the time goes:
time: 753 us; the launch traced here: 748 us
  blocking collectives  633 us (84%)
  matrix products  54.8 us (7%)
  starting transfers between devices  27.5 us (4%)
  other arithmetic  17 us (2%)
  local copies, waits for them, and re-layouts  14.1 us (2%)
    all_gather x4, blocking collectives, precondition(): lax.all_gather(coefficients, ('row', 'col'), axis=1, tiled=True)  252 us
    psum x3, blocking collectives, pair_totals(): lax.psum((jnp.sum(first_field * second_field, axis=1), jnp.sum(third_fiel...  232 us
    psum x2, blocking collectives, shards(): cross_sum = lax.psum(jnp.sum(correction * image, axis=1), ('row', 'col'))  149 us
    dot_general x6, matrix products, sparse_forward(): product = jnp.einsum('lbkw,bkwv->lbv', picked, tile_set, precision=PRECISE)  23.5 us
    dot_general x6, matrix products, sparse_backward(): product = jnp.einsum('lbv,bkwv->lbkw', pieces, tile_set, precision=PRECISE)  21.4 us
    ppermute x6, starting transfers between devices, with_halo(): lax.ppermute(tail, axis, [(i, (i + 1) % count) for i in range(ends)])  16.4 us
  transfers between devices with their start and end apart: 12, of which 0 were waited for; matrix products, arithmetic and copies ran while one was open for 7% of the time, Pallas kernels for 0%

commit v1 on v0

--- a/solution.py
+++ b/solution.py
@@ -5,6 +5,11 @@
 
 ITERS = 3
 PRECISE = lax.Precision.HIGHEST
+
+
+def exchange_gather(shard, axis, along):
+    repeated = jnp.stack([shard] * lax.axis_size(axis))
+    return jnp.concatenate(lax.all_to_all(repeated, axis, 0, 0), axis=along)
 
 
 def with_halo(cells, sides, width):
@@ -95,7 +100,7 @@
         coefficients = jnp.einsum("lm,dm->ld", vector, deflation, precision=PRECISE)
         energy = jnp.einsum(
             "ln,dn->ld",
-            lax.all_gather(coefficients, ("row", "col"), axis=1, tiled=True),
+            exchange_gather(coefficients, ("row", "col"), 1),
             coarse_rows,
             precision=PRECISE,
         )

time: 753 us -> 617 us (0.82)
  blocking collectives: 633 us -> 444 us
  starting transfers between devices: 27.5 us -> 45 us
  other arithmetic: 17 us -> 29.2 us
  waiting for transfers between devices: 0.03 us -> 11.3 us
  local copies, waits for them, and re-layouts: 14.1 us -> 22.8 us
    all_gather x4 -> x0, blocking collectives: 252 us -> none  [precondition(): lax.all_gather(coefficients, ('row', 'col'), axis=1, tiled=True)]
    all_to_all x0 -> x3, blocking collectives: none -> 68 us  [exchange_gather(): return jnp.concatenate(lax.all_to_all(repeated, axis, 0, 0), axis=along)]
    all_to_all x0 -> x1, starting transfers between devices: none -> 15.6 us  [exchange_gather(): return jnp.concatenate(lax.all_to_all(repeated, axis, 0, 0), axis=along)]
    all_to_all x0 -> x1, waiting for transfers between devices: none -> 11.3 us  [exchange_gather(): return jnp.concatenate(lax.all_to_all(repeated, axis, 0, 0), axis=along)]
  transfers between devices with their start and end apart: 12 -> 13, of which waited for: 0 -> 1; matrix products, arithmetic and copies ran while one was open for 7% -> 10% of each run, Pallas kernels for 0% -> 0%
where the time goes in v1:
time: 617 us; the launch traced here: 611 us
  blocking collectives  444 us (72%)
  matrix products  57.5 us (9%)
  starting transfers between devices  45 us (7%)
  other arithmetic  29.2 us (5%)
  local copies, waits for them, and re-layouts  22.8 us (4%)
  waiting for transfers between devices  11.3 us (2%)
    psum x3, blocking collectives, pair_totals(): lax.psum((jnp.sum(first_field * second_field, axis=1), jnp.sum(third_fiel...  230 us
    psum x2, blocking collectives, shards(): cross_sum = lax.psum(jnp.sum(correction * image, axis=1), ('row', 'col'))  145 us
    all_to_all x3, blocking collectives, exchange_gather(): return jnp.concatenate(lax.all_to_all(repeated, axis, 0, 0), axis=along)  68 us
    dot_general x6, matrix products, sparse_forward(): product = jnp.einsum('lbkw,bkwv->lbv', picked, tile_set, precision=PRECISE)  23.5 us
    dot_general x6, matrix products, sparse_backward(): product = jnp.einsum('lbv,bkwv->lbkw', pieces, tile_set, precision=PRECISE)  21.4 us
    ppermute x6, starting transfers between devices, with_halo(): lax.ppermute(tail, axis, [(i, (i + 1) % count) for i in range(ends)])  18.7 us
    all_to_all x1, starting transfers between devices, exchange_gather(): return jnp.concatenate(lax.all_to_all(repeated, axis, 0, 0), axis=along)  15.6 us
  transfers between devices with their start and end apart: 13, of which 1 were waited for; matrix products, arithmetic and copies ran while one was open for 10% of the time, Pallas kernels for 0%

profile of v1, /device:TPU:1, one launch (start us, length us, event | category | flops | bytes accessed | tf_op | source)
XLA Modules:
  0.0 611.5 jit_solution(11242831021035833095)
XLA Ops:
  0.6 1.3 fusion.36
  2.1 1.1 reshape.361
  3.3 15.6 %all-to-all-start = ((f32[256,1,256]{2,1,0:T(1,128)}), f32[256,1,256]{2,1,0:T(1,128)S(1)}, u32[]{:S(2)}, u32[]{:S(2)}) async-start(f32[256,1,256]{2,1,0:T(1,128)} %reshape.361), calls=%async_computation | async-start | bytes 524288 | tf_op jit(solution)/shard_map/all_to_all | solution.py:12
  20.3 0.8 copy.48
  21.2 0.8 copy.47
  23.6 11.3 %all-to-all-done = f32[256,1,256]{2,1,0:T(1,128)S(1)} async-done(((f32[256,1,256]{2,1,0:T(1,128)}), f32[256,1,256]{2,1,0:T(1,128)S(1)}, u32[]{:S(2)}, u32[]{:S(2)}) %all-to-all-start) | async-done | bytes 262176 | tf_op jit(solution)/shard_map/all_to_all | solution.py:12
  35.4 1.3 reduce
  37.7 0.9 fusion.37
  39.2 1.0 gather_fusion.2
  40.5 1.3 collective-permute-start
  41.9 1.3 collective-permute-start.1
  43.2 4.2 collective-permute-start.2
  47.5 2.2 collective-permute-start.3
  50.5 3.8 convolution_bitcast_fusion.17
  55.2 4.0 convolution_bitcast_fusion.16
  59.2 3.6 convolution_bitcast_fusion.5
  63.2 3.6 convolution_bitcast_fusion.4
  68.0 4.2 scatter_custom_fusion
  72.7 76.3 %all-reduce.2 = (f32[8]{0:T(128)S(1)}, f32[8]{0:T(128)S(1)}) all-reduce(f32[8]{0:T(128)S(1)} %get-tuple-element.10, f32[8]{0:T(128)S(1)} %get-tuple-element.9), channel_id=1, replica_groups=mesh['row'=16,'col'=16] {'row','col'}, use_global_device_ids=true, to_apply=%region_1.2 | all-reduce | flops 16 | bytes 128 | tf_op jit(solution)/shard_map/psum | solution.py:58
  151.0 22.4 %all_to_all.20 = f32[256,1,256]{2,1,0:T(1,128)S(1)} all-to-all(f32[256,1,256]{2,1,0:T(1,128)S(1)} %reshape.363), channel_id=1, replica_groups=mesh['row'=16,'col'=16] {'row','col'}, dimensions={0} | all-to-all | bytes 524288 | tf_op jit(solution)/shard_map/all_to_all | solution.py:12
  173.3 1.3 reduce.1
  175.6 0.9 fusion.39
  176.5 1.2 multiply_reduce_fusion.5
  177.7 72.7 %psum.58 = f32[8]{0:T(128)S(1)} all-reduce(f32[8]{0:T(128)S(1)} %get-tuple-element.31), channel_id=1, replica_groups=mesh['row'=16,'col'=16] {'row','col'}, use_global_device_ids=true, to_apply=%region_6.9 | all-reduce | flops 8 | bytes 64 | tf_op jit(solution)/shard_map/psum | solution.py:121
  251.5 1.0 gather_fusion.5
  253.3 2.2 collective-permute-start.4
  255.6 1.3 collective-permute-start.5
  257.0 4.5 collective-permute-start.6
  261.6 2.1 collective-permute-start.7
  263.7 0.8 gather_fusion.3
  264.4 0.8 broadcast_select_fusion.6
  265.2 3.8 convolution_bitcast_fusion.15
  269.1 0.8 gather_fusion.4
  270.0 4.0 convolution_bitcast_fusion.14
  274.0 3.6 convolution_bitcast_fusion.3
  278.0 3.6 convolution_bitcast_fusion.2
  282.8 4.0 scatter_custom_fusion.1
  287.3 77.0 %all-reduce.1 = (f32[8]{0:T(128)S(1)}, f32[8]{0:T(128)S(1)}) all-reduce(f32[8]{0:T(128)S(1)} %get-tuple-element.8, f32[8]{0:T(128)S(1)} %get-tuple-element.7), channel_id=1, replica_groups=mesh['row'=16,'col'=16] {'row','col'}, use_global_device_ids=true, to_apply=%region_8.11 | all-reduce | flops 16 | bytes 128 | tf_op jit(solution)/shard_map/psum | solution.py:58
  365.5 1.1 fusion.40
  367.2 22.8 %all_to_all.21 = f32[256,1,256]{2,1,0:T(1,128)S(1)} all-to-all(f32[256,1,256]{2,1,0:T(1,128)S(1)} %reshape.365), channel_id=1, replica_groups=mesh['row'=16,'col'=16] {'row','col'}, dimensions={0} | all-to-all | bytes 524288 | tf_op jit(solution)/shard_map/all_to_all | solution.py:12
  390.0 1.3 reduce.2
  392.3 0.9 fusion.41
  393.2 1.2 multiply_reduce_fusion.2
  394.4 72.7 %psum.61 = f32[8]{0:T(128)S(1)} all-reduce(f32[8]{0:T(128)S(1)} %get-tuple-element.33), channel_id=1, replica_groups=mesh['row'=16,'col'=16] {'row','col'}, use_global_device_ids=true, to_apply=%region_13.16 | all-reduce | flops 8 | bytes 64 | tf_op jit(solution)/shard_map/psum | solution.py:121
  468.2 1.0 gather_fusion.8
  470.1 4.2 collective-permute-start.10
  474.4 1.9 collective-permute-start.11
  476.3 2.2 collective-permute-start.8
  478.6 1.7 collective-permute-start.9
  480.3 0.8 gather_fusion.6
  481.1 0.8 broadcast_select_fusion.4
  481.9 3.8 convolution_bitcast_fusion.13
  485.8 0.8 gather_fusion.7
  486.7 4.0 convolution_bitcast_fusion.12
  490.7 3.6 convolution_bitcast_fusion.1
  494.7 3.6 convolution_bitcast_fusion
  499.4 4.0 scatter_custom_fusion.2
  503.7 1.0 multiply_reduce_fusion
  504.8 77.2 %all-reduce = (f32[8]{0:T(128)S(1)}, f32[8]{0:T(128)S(1)}) all-reduce(f32[8]{0:T(128)S(1)} %get-tuple-element.6, f32[8]{0:T(128)S(1)} %get-tuple-element.5), channel_id=1, replica_groups=mesh['row'=16,'col'=16] {'row','col'}, use_global_device_ids=true, to_apply=%region_15.18 | all-reduce | flops 16 | bytes 128 | tf_op jit(solution)/shard_map/psum | solution.py:58
  582.0 1.6 multiply_subtract_fusion
  584.4 22.8 %all_to_all.22 = f32[256,1,256]{2,1,0:T(1,128)S(1)} all-to-all(f32[256,1,256]{2,1,0:T(1,128)S(1)} %reshape.367), channel_id=1, replica_groups=mesh['row'=16,'col'=16] {'row','col'}, dimensions={0} | all-to-all | bytes 524288 | tf_op jit(solution)/shard_map/all_to_all | solution.py:12
  607.2 1.3 reduce.3
  609.5 0.9 fusion.43
  610.4 0.9 convolution_add_fusion
  (171 shorter events, 24.7 us)
Async XLA Ops:
  0.6 37.1 %copy-start = (f32[32,8192]{1,0:T(8,128)S(1)}, f32[32,8192]{1,0:T(8,128)}, u32[]{:S(2)}) copy-start(f32[32,8192]{1,0:T(8,128)} %param.19) | copy-start | bytes 3145732
  2.1 36.5 %copy-start.7 = (f32[32,2048]{1,0:T(8,128)S(1)}, f32[32,2048]{1,0:T(8,128)}, u32[]{:S(2)}) copy-start(f32[32,2048]{1,0:T(8,128)} %param.18) | copy-start | bytes 786436
  2.1 36.5 %copy-start.8 = (f32[8,2048]{1,0:T(8,128)S(1)}, f32[8,2048]{1,0:T(8,128)}, u32[]{:S(2)}) copy-start(f32[8,2048]{1,0:T(8,128)} %param.13) | copy-start | bytes 196612
  3.3 31.6 %all-to-all-start = ((f32[256,1,256]{2,1,0:T(1,128)}), f32[256,1,256]{2,1,0:T(1,128)S(1)}, u32[]{:S(2)}, u32[]{:S(2)}) async-start(f32[256,1,256]{2,1,0:T(1,128)} %reshape.361), calls=%async_computation | async-start | bytes 524288 | tf_op jit(solution)/shard_map/all_to_all | solution.py:12
  20.3 47.4 %copy-start.14 = (pred[512]{0:T(512)(128)(4,1)}, pred[512]{0:T(512)(128)(4,1)S(1)}, u32[]{:S(2)}) copy-start(pred[512]{0:T(512)(128)(4,1)S(1)} %compare_and_fusion) | copy-start | bytes 1540
  21.2 29.2 %copy-start.22 = (pred[64]{0:T(512)(128)(4,1)}, pred[64]{0:T(512)(128)(4,1)S(1)}, u32[]{:S(2)}) copy-start(pred[64]{0:T(512)(128)(4,1)S(1)} %compare_and_fusion.2) | copy-start | bytes 196
  22.1 33.0 %copy-start.19 = (pred[64]{0:T(512)(128)(4,1)}, pred[64]{0:T(512)(128)(4,1)S(1)}, u32[]{:S(2)}) copy-start(pred[64]{0:T(512)(128)(4,1)S(1)} %compare_and_fusion.1) | copy-start | bytes 196
  22.1 27.6 %copy-start.18 = (s32[1024]{0:T(1024)}, s32[1024]{0:T(1024)S(1)}, u32[]{:S(2)}) copy-start(s32[1024]{0:T(1024)S(1)} %pad_clamp_fusion.2) | copy-start | bytes 12292
  22.1 32.3 %copy-start.17 = (s32[1024]{0:T(1024)}, s32[1024]{0:T(1024)S(1)}, u32[]{:S(2)}) copy-start(s32[1024]{0:T(1024)S(1)} %pad_clamp_fusion.1) | copy-start | bytes 12292
  23.6 44.4 %copy-start.23 = (s32[512,1]{0,1:T(1,128)}, s32[512,1]{0,1:T(1,128)S(1)}, u32[]{:S(2)}) copy-start(s32[512,1]{0,1:T(1,128)S(1)} %compare_select_fusion) | copy-start | bytes 6148
  40.5 27.1 %collective-permute-start = (f32[8,1,128]{2,0,1:T(8,128)S(1)}, f32[8,1,128]{2,0,1:T(8,128)S(1)}, u32[]{:S(2)}, u32[]{:S(2)}) collective-permute-start(f32[8,1,128]{2,0,1:T(8,128)S(1)} %copy.114), channel_id=1, source_target_pairs={{0,16},{16,32},{32,48},{48,64},{64,80},{80,96},{96,112},{112,128},... | collective-permute-start | bytes 12296 | tf_op jit(solution)/shard_map/ppermute | solution.py:23
  41.9 25.7 %collective-permute-start.1 = (f32[8,1,128]{2,0,1:T(8,128)S(1)}, f32[8,1,128]{2,0,1:T(8,128)S(1)}, u32[]{:S(2)}, u32[]{:S(2)}) collective-permute-start(f32[8,1,128]{2,0,1:T(8,128)S(1)} %copy.115), channel_id=1, source_target_pairs={{16,0},{32,16},{48,32},{64,48},{80,64},{96,80},{112,96},{128,112},... | collective-permute-start | bytes 12296 | tf_op jit(solution)/shard_map/ppermute | solution.py:25
  43.2 24.4 %collective-permute-start.2 = (f32[8,1,128]{2,0,1:T(8,128)S(1)}, f32[8,1,128]{2,0,1:T(8,128)S(1)}, u32[]{:S(2)}, u32[]{:S(2)}) collective-permute-start(f32[8,1,128]{2,0,1:T(8,128)S(1)} %copy.116), channel_id=1, source_target_pairs={{0,1},{1,2},{2,3},{3,4},{4,5},{5,6},{6,7},{7,8},{8,9},{9,10},{10,1... | collective-permute-start | bytes 12296 | tf_op jit(solution)/shard_map/ppermute | solution.py:23
  47.5 20.1 %collective-permute-start.3 = (f32[8,1,128]{2,0,1:T(8,128)S(1)}, f32[8,1,128]{2,0,1:T(8,128)S(1)}, u32[]{:S(2)}, u32[]{:S(2)}) collective-permute-start(f32[8,1,128]{2,0,1:T(8,128)S(1)} %copy.117), channel_id=1, source_target_pairs={{1,0},{2,1},{3,2},{4,3},{5,4},{6,5},{7,6},{8,7},{9,8},{10,9},{11,1... | collective-permute-start | bytes 12296 | tf_op jit(solution)/shard_map/ppermute | solution.py:25
  55.0 4.2 copy-start.1
  55.2 7.6 %copy-start.12 = (s32[16,4]{0,1:T(4,128)S(1)}, s32[16,4]{0,1:T(4,128)}, u32[]{:S(2)}) copy-start(s32[16,4]{0,1:T(4,128)} %param.17) | copy-start | bytes 772
  55.2 8.0 %copy-start.4 = (f32[8192,128]{1,0:T(8,128)S(1)}, f32[8192,128]{1,0:T(8,128)}, u32[]{:S(2)}) copy-start(f32[8192,128]{1,0:T(8,128)} %param.14) | copy-start | bytes 12582916
  59.2 7.6 %copy-start.13 = (s32[16,4]{0,1:T(4,128)S(1)}, s32[16,4]{0,1:T(4,128)}, u32[]{:S(2)}) copy-start(s32[16,4]{0,1:T(4,128)} %param.15) | copy-start | bytes 772
  72.5 77.8 %copy-start.10 = (f32[8,2048]{1,0:T(8,128)}, f32[8,2048]{1,0:T(8,128)S(1)}, u32[]{:S(2)}) copy-start(f32[8,2048]{1,0:T(8,128)S(1)} %copy.59) | copy-start | bytes 196612
  149.0 0.5 copy-start.29
  149.5 0.5 copy-start.24
  251.2 18.7 %copy-start.20 = (pred[64]{0:T(512)(128)(4,1)S(1)}, pred[64]{0:T(512)(128)(4,1)}, u32[]{:S(2)}) copy-start(pred[64]{0:T(512)(128)(4,1)} %copy-done.19) | copy-start | bytes 196
  253.3 29.0 %collective-permute-start.4 = (f32[8,1,128]{2,0,1:T(8,128)S(1)}, f32[8,1,128]{2,0,1:T(8,128)S(1)}, u32[]{:S(2)}, u32[]{:S(2)}) collective-permute-start(f32[8,1,128]{2,0,1:T(8,128)S(1)} %copy.118), channel_id=1, source_target_pairs={{0,16},{16,32},{32,48},{48,64},{64,80},{80,96},{96,112},{112,128},... | collective-permute-start | bytes 12296 | tf_op jit(solution)/shard_map/ppermute | solution.py:23
  255.6 26.8 %collective-permute-start.5 = (f32[8,1,128]{2,0,1:T(8,128)S(1)}, f32[8,1,128]{2,0,1:T(8,128)S(1)}, u32[]{:S(2)}, u32[]{:S(2)}) collective-permute-start(f32[8,1,128]{2,0,1:T(8,128)S(1)} %copy.119), channel_id=1, source_target_pairs={{16,0},{32,16},{48,32},{64,48},{80,64},{96,80},{112,96},{128,112},... | collective-permute-start | bytes 12296 | tf_op jit(solution)/shard_map/ppermute | solution.py:25
  257.0 25.4 %collective-permute-start.6 = (f32[8,1,128]{2,0,1:T(8,128)S(1)}, f32[8,1,128]{2,0,1:T(8,128)S(1)}, u32[]{:S(2)}, u32[]{:S(2)}) collective-permute-start(f32[8,1,128]{2,0,1:T(8,128)S(1)} %copy.120), channel_id=1, source_target_pairs={{0,1},{1,2},{2,3},{3,4},{4,5},{5,6},{6,7},{7,8},{8,9},{9,10},{10,1... | collective-permute-start | bytes 12296 | tf_op jit(solution)/shard_map/ppermute | solution.py:23
  261.6 20.8 %collective-permute-start.7 = (f32[8,1,128]{2,0,1:T(8,128)S(1)}, f32[8,1,128]{2,0,1:T(8,128)S(1)}, u32[]{:S(2)}, u32[]{:S(2)}) collective-permute-start(f32[8,1,128]{2,0,1:T(8,128)S(1)} %copy.121), channel_id=1, source_target_pairs={{1,0},{2,1},{3,2},{4,3},{5,4},{6,5},{7,6},{8,7},{9,8},{10,9},{11,1... | collective-permute-start | bytes 12296 | tf_op jit(solution)/shard_map/ppermute | solution.py:25
  269.9 4.2 copy-start.2
  270.0 8.0 %copy-start.5 = (f32[8192,128]{1,0:T(8,128)S(1)}, f32[8192,128]{1,0:T(8,128)}, u32[]{:S(2)}) copy-start(f32[8192,128]{1,0:T(8,128)} %param.14) | copy-start | bytes 12582916
  277.6 4.9 copy-start.15
  287.1 79.5 %copy-start.9 = (f32[8,2048]{1,0:T(8,128)}, f32[8,2048]{1,0:T(8,128)S(1)}, u32[]{:S(2)}) copy-start(f32[8,2048]{1,0:T(8,128)S(1)} %copy.73) | copy-start | bytes 196612
  364.3 2.4 copy-start.28
  364.3 0.5 copy-start.26
  467.9 18.6 %copy-start.21 = (pred[64]{0:T(512)(128)(4,1)S(1)}, pred[64]{0:T(512)(128)(4,1)}, u32[]{:S(2)}) copy-start(pred[64]{0:T(512)(128)(4,1)} %copy-done.19) | copy-start | bytes 196
  470.1 29.0 %collective-permute-start.10 = (f32[8,1,128]{2,0,1:T(8,128)S(1)}, f32[8,1,128]{2,0,1:T(8,128)S(1)}, u32[]{:S(2)}, u32[]{:S(2)}) collective-permute-start(f32[8,1,128]{2,0,1:T(8,128)S(1)} %copy.124), channel_id=1, source_target_pairs={{0,1},{1,2},{2,3},{3,4},{4,5},{5,6},{6,7},{7,8},{8,9},{9,10},{10,1... | collective-permute-start | bytes 12296 | tf_op jit(solution)/shard_map/ppermute | solution.py:23
  474.4 24.7 %collective-permute-start.11 = (f32[8,1,128]{2,0,1:T(8,128)S(1)}, f32[8,1,128]{2,0,1:T(8,128)S(1)}, u32[]{:S(2)}, u32[]{:S(2)}) collective-permute-start(f32[8,1,128]{2,0,1:T(8,128)S(1)} %copy.125), channel_id=1, source_target_pairs={{1,0},{2,1},{3,2},{4,3},{5,4},{6,5},{7,6},{8,7},{9,8},{10,9},{11,1... | collective-permute-start | bytes 12296 | tf_op jit(solution)/shard_map/ppermute | solution.py:25
  476.3 22.7 %collective-permute-start.8 = (f32[8,1,128]{2,0,1:T(8,128)S(1)}, f32[8,1,128]{2,0,1:T(8,128)S(1)}, u32[]{:S(2)}, u32[]{:S(2)}) collective-permute-start(f32[8,1,128]{2,0,1:T(8,128)S(1)} %copy.122), channel_id=1, source_target_pairs={{0,16},{16,32},{32,48},{48,64},{64,80},{80,96},{96,112},{112,128},... | collective-permute-start | bytes 12296 | tf_op jit(solution)/shard_map/ppermute | solution.py:23
  478.6 20.5 %collective-permute-start.9 = (f32[8,1,128]{2,0,1:T(8,128)S(1)}, f32[8,1,128]{2,0,1:T(8,128)S(1)}, u32[]{:S(2)}, u32[]{:S(2)}) collective-permute-start(f32[8,1,128]{2,0,1:T(8,128)S(1)} %copy.123), channel_id=1, source_target_pairs={{16,0},{32,16},{48,32},{64,48},{80,64},{96,80},{112,96},{128,112},... | collective-permute-start | bytes 12296 | tf_op jit(solution)/shard_map/ppermute | solution.py:25
  486.5 4.2 copy-start.3
  486.7 8.0 %copy-start.6 = (f32[8192,128]{1,0:T(8,128)S(1)}, f32[8192,128]{1,0:T(8,128)}, u32[]{:S(2)}) copy-start(f32[8192,128]{1,0:T(8,128)} %param.14) | copy-start | bytes 12582916
  494.3 5.0 copy-start.16
  494.7 87.3 %copy-start.25 = (f32[8]{0:T(128)S(1)}, f32[8]{0:T(128)}, u32[]{:S(2)}) copy-start(f32[8]{0:T(128)} %copy-done.24) | copy-start | bytes 100
  494.7 87.3 %copy-start.27 = (f32[8]{0:T(128)S(1)}, f32[8]{0:T(128)}, u32[]{:S(2)}) copy-start(f32[8]{0:T(128)} %copy-done.26) | copy-start | bytes 100
  583.5 26.9 %copy-start.11 = (f32[8,2048]{1,0:T(8,128)}, f32[8,2048]{1,0:T(8,128)S(1)}, u32[]{:S(2)}) copy-start(f32[8,2048]{1,0:T(8,128)S(1)} %get-tuple-element.29) | copy-start | bytes 196612
